TPU v7x, 256 devices: a whole 4x4x8 slice. The times are simulated.
256 devices in a mesh: seq: 32 (over z, y), uly: 8 (over x, core).
Axes of the slice: x: 4, y: 4, z: 8, core: 2. Of those that a mesh axis runs over, the one named last changes fastest.
Arguments:
- queries: bfloat16 [32768, 5120], P(('seq', 'uly')), may hold values from -27 to 27
- keys: bfloat16 [32768, 5120], P(('seq', 'uly')), may hold values from -9 to 9
- values: bfloat16 [32768, 5120], P(('seq', 'uly')), may hold values from -6 to 6
- block_lists: int32 [256, 12], P('seq'), may hold values from 0 to 255, as said below
- block_counts: int32 [256], P('seq'), may hold values from 4 to 12
Outputs:
- attended: bfloat16 [32768, 5120], P(('seq', 'uly'))
Inputs may be any that keep to these rules, and one draw needn't show every extreme that they name: `block_lists`: each row names 12 different blocks, its first entry being the query block itself; only the first block_counts entries of a row are used, the rest are block numbers too. Over the used entries of the 8 query blocks of one group (blocks g * 8 to (g + 1) * 8 - 1), at most 2 different blocks of any other group are named, and in every group exactly 2 of some other group.
All inputs are finite; a program needn't handle non-finite values.
Results may differ from a plain program's by a relative error of at most 0.003.
Values may be sent and summed in bfloat16 or wider, within the bound.
A program may use at most 128 MiB of HBM per device.

v0:
```python
import jax
import jax.numpy as jnp
from jax import lax
from jax.sharding import PartitionSpec as P

HEAD_DIM = 128
BLOCK_LEN = 128
LIST_LEN = 12
PEER_SLOTS = 2


def finish(scores, value_part, block_count, entry_ids):
    live_keys = jnp.repeat(entry_ids < block_count, BLOCK_LEN)
    scores = jnp.where(live_keys[None, None, :], scores, -jnp.inf)
    row_max = jnp.max(scores, axis=2, keepdims=True)
    weights = jnp.exp(scores - row_max)
    weight_sum = jnp.sum(weights, axis=2)
    blended = jnp.einsum(
        "hqk,khd->qhd", weights.astype(jnp.bfloat16), value_part, preferred_element_type=jnp.float32
    )
    result = blended / jnp.transpose(weight_sum)[:, :, None]
    return result.astype(jnp.bfloat16)


def body(queries, keys, values, block_lists, block_counts):
    q_heads, k_heads, v_heads = (
        lax.all_to_all(queries, "uly", split_axis=1, concat_axis=0, tiled=True),
        lax.all_to_all(keys, "uly", split_axis=1, concat_axis=0, tiled=True),
        lax.all_to_all(values, "uly", split_axis=1, concat_axis=0, tiled=True),
    )
    row_count, feat_width = q_heads.shape
    group_blocks = row_count // BLOCK_LEN
    groups = lax.axis_size("seq")
    my_group = lax.axis_index("seq")
    head_count = feat_width // HEAD_DIM
    total_blocks = groups * group_blocks
    kv_pairs = jnp.concatenate([k_heads, v_heads], axis=1).reshape(
        group_blocks, BLOCK_LEN, 2 * feat_width
    )
    entry_ids = jnp.arange(LIST_LEN, dtype=jnp.int32)
    live_entry = entry_ids[None, :] < block_counts[:, None]
    block_ids = jnp.arange(total_blocks, dtype=jnp.int32)
    matches = block_lists[:, :, None] == block_ids[None, None, :]
    owners = block_ids // group_blocks
    remote = owners != my_group
    needed = (jnp.any(matches & live_entry[:, :, None], axis=(0, 1)) & remote).astype(jnp.int32)
    needed = needed.reshape(groups, group_blocks)
    asked_for = lax.all_to_all(needed, "seq", split_axis=0, concat_axis=0, tiled=True)
    ask_rank = jnp.cumsum(asked_for, axis=1) - 1
    slot_ids = jnp.arange(PEER_SLOTS, dtype=jnp.int32)
    chosen = (asked_for[:, None, :] == 1) & (ask_rank[:, None, :] == slot_ids[None, :, None])
    picked = jnp.sum(
        chosen.astype(jnp.int32) * jnp.arange(group_blocks, dtype=jnp.int32)[None, None, :], axis=2
    )
    outgoing = jnp.take(kv_pairs, picked.reshape(-1), axis=0).reshape(
        groups, PEER_SLOTS, BLOCK_LEN, 2 * feat_width
    )
    arrived = lax.all_to_all(outgoing, "seq", split_axis=0, concat_axis=0, tiled=True)
    pool = jnp.concatenate(
        [kv_pairs, arrived.reshape(groups * PEER_SLOTS, BLOCK_LEN, 2 * feat_width)], axis=0
    )
    need_rank = (jnp.cumsum(needed, axis=1) - 1).reshape(-1)
    slot_table = jnp.where(
        remote, group_blocks + owners * PEER_SLOTS + need_rank, block_ids % group_blocks
    )
    entry_slot = jnp.sum(matches.astype(jnp.int32) * slot_table[None, None, :], axis=2)
    entry_slot = jnp.clip(entry_slot, 0, pool.shape[0] - 1)
    q_blocks = q_heads.reshape(group_blocks, BLOCK_LEN, head_count, HEAD_DIM)
    score_scale = HEAD_DIM ** (-0.5)

    def attend(inputs):
        q_block, slot_list, block_count = inputs
        gathered = jnp.take(pool, slot_list, axis=0).reshape(
            LIST_LEN * BLOCK_LEN, 2, head_count, HEAD_DIM
        )
        scores = (
            jnp.einsum("qhd,khd->hqk", q_block, gathered[:, 0], preferred_element_type=jnp.float32)
            * score_scale
        )
        result = finish(scores, gathered[:, 1], block_count, entry_ids)
        return result.reshape(BLOCK_LEN, head_count * HEAD_DIM)

    attended = lax.map(attend, (q_blocks, entry_slot, block_counts))
    return lax.all_to_all(
        attended.reshape(row_count, feat_width), "uly", split_axis=0, concat_axis=1, tiled=True
    )


def solution(mesh):
    placed = (
        P(("seq", "uly"), None),
        P(("seq", "uly"), None),
        P(("seq", "uly"), None),
        P("seq", None),
        P("seq"),
    )
    return jax.shard_map(
        body, mesh=mesh, in_specs=placed, out_specs=P(("seq", "uly"), None), check_vma=False
    )
```

profile of v0, /device:TPU:96, one launch (start us, length us, event | category | flops | bytes accessed | tf_op | source)
XLA Modules:
  0.0 931.4 jit_solution(10417599941408593023)
XLA Ops:
  2.4 10.5 %all-to-all-start.2 = ((s32[32,1,8]{2,1,0:T(1,128)}), s32[32,1,8]{2,1,0:T(1,128)S(1)}, u32[]{:S(2)}, u32[]{:S(2)}) async-start(s32[32,1,8]{2,1,0:T(1,128)} %bitcast.4), calls=%async_computation.2 | async-start | bytes 32768 | tf_op jit(solution)/shard_map/all_to_all | solution.py:48
  12.8 2.4 copy.34
  15.3 4.3 all-to-all-done.2
  19.6 4.3 all-to-all-start
  25.4 17.3 %all-to-all-done = bf16[128,8,640]{0,2,1:T(8,128)(2,1)S(1)} async-done(((bf16[128,8,640]{0,2,1:T(8,128)(2,1)}), bf16[128,8,640]{0,2,1:T(8,128)(2,1)S(1)}, u32[]{:S(2)}, u32[]{:S(2)}) %all-to-all-start) | async-done | bytes 1310752 | tf_op jit(solution)/shard_map/all_to_all | solution.py:28
  42.7 3.6 all-to-all-start.1
  47.0 18.0 %all-to-all-done.1 = bf16[128,8,640]{0,2,1:T(8,128)(2,1)S(1)} async-done(((bf16[128,8,640]{0,2,1:T(8,128)(2,1)}), bf16[128,8,640]{0,2,1:T(8,128)(2,1)S(1)}, u32[]{:S(2)}, u32[]{:S(2)}) %all-to-all-start.1) | async-done | bytes 1310752 | tf_op jit(solution)/shard_map/all_to_all | solution.py:29
  66.0 1.9 pad_maximum_fusion.1
  67.9 8.9 gather_fusion.1
  76.8 17.7 %broadcast_select_fusion = bf16[32,2,128,1280]{2,3,1,0:T(8,128)(2,1)} fusion(bf16[32,2,128,1280]{2,3,1,0:T(8,128)(2,1)} %bitcast.84, pred[32,2]{1,0:T(8,128)(4,1)S(1)} %copy.40), kind=kLoop, calls=%fused_computation.29 | loop fusion | flops 10485760 | bytes 41943104 | tf_op jit(solution)/shard_map/jit(_take)/select_n | solution.py:55
  94.4 8.0 all-to-all-start.3
  103.3 2.5 copy.44
  105.8 2.6 copy.43
  108.4 491.0 %all-to-all-done.3 = bf16[32,2,128,1280]{2,3,1,0:T(8,128)(2,1)} async-done(((bf16[32,2,128,1280]{2,3,1,0:T(8,128)(2,1)}), bf16[32,2,128,1280]{2,3,1,0:T(8,128)(2,1)}, u32[]{:S(2)}, u32[]{:S(2)}) %all-to-all-start.3) | async-done | bytes 20971552 | tf_op jit(solution)/shard_map/all_to_all | solution.py:58
  599.3 14.1 %all-to-all-start.4 = ((bf16[128,8,640]{0,2,1:T(8,128)(2,1)}), bf16[128,8,640]{0,2,1:T(8,128)(2,1)}, u32[]{:S(2)}, u32[]{:S(2)}) async-start(bf16[128,8,640]{0,2,1:T(8,128)(2,1)} %bitcast.88), calls=%async_computation.4 | async-start | bytes 2621440 | tf_op jit(solution)/shard_map/all_to_all | solution.py:27
  613.4 27.3 %copy.42 = bf16[32,2,128,1280]{3,2,1,0:T(8,128)(2,1)} copy(bf16[32,2,128,1280]{2,3,1,0:T(8,128)(2,1)} %all-to-all-done.3) | data formatting | bytes 41943040 | tf_op jit(solution)/shard_map/all_to_all | solution.py:58
  640.8 19.8 %pad_maximum_fusion = bf16[72,128,1280]{2,1,0:T(8,128)(2,1)} fusion(bf16[64,128,1280]{2,1,0:T(8,128)(2,1)} %bitcast.83, bf16[8,128,1280]{2,1,0:T(8,128)(2,1)S(1)} %copy-done), kind=kLoop, calls=%fused_computation.28 | loop fusion | flops 11796480 | bytes 47185920 | tf_op jit(solution)/shard_map/concatenate | solution.py:59
  660.6 245.8 %while.11 = (s32[]{:T(128)}, bf16[8,128,640]{1,2,0:T(8,128)(2,1)}, s32[8,12]{1,0:T(8,128)S(1)}, bf16[72,128,1280]{2,1,0:T(8,128)(2,1)}, s32[8]{0:T(128)S(1)}, /*index=5*/bf16[8,128,5,128]{1,3,2,0:T(8,128)(2,1)}, s32[]{:T(128)}) while((s32[]{:T(128)}, bf16[8,128,640]{1,2,0:T(8,128)(2,1)}, s32[8,12]{1,0:T(8,128)S(1)}, ...), condition=%wide.region_8.9_spmd.clone, body=%wide.region_5.8_spmd.clone.sunk | while | flops 512327552 | bytes 40004996 | solution.py:83
  660.6 10.5 %gather_fusion = bf16[12,128,1280]{2,1,0:T(8,128)(2,1)} fusion(bf16[72,128,1280]{2,1,0:T(8,128)(2,1)} %get-tuple-element.147, s32[1024]{0:T(1024)S(1)} %pad_clamp_fusion.3), kind=kCustom, calls=%fused_computation.clone.clone.1 | custom fusion | bytes 7864368 | tf_op jit(solution)/shard_map/while/body/eval_jaxpr/jit(_take)/gather | solution.py:73
  671.1 9.6 %reshape.292 = bf16[1536,2,5,128]{3,2,1,0:T(8,128)(2,1)} reshape(bf16[12,128,1280]{2,1,0:T(8,128)(2,1)} %gather_fusion) | data formatting | bytes 7864320 | tf_op jit(solution)/shard_map/while/body/eval_jaxpr/jit(_take)/gather | solution.py:73
  680.8 4.9 copy_select_fusion.2
  691.4 10.5 %gather_fusion = bf16[12,128,1280]{2,1,0:T(8,128)(2,1)} fusion(bf16[72,128,1280]{2,1,0:T(8,128)(2,1)} %get-tuple-element.147, s32[1024]{0:T(1024)S(1)} %pad_clamp_fusion.3), kind=kCustom, calls=%fused_computation.clone.clone.1 | custom fusion | bytes 7864368 | tf_op jit(solution)/shard_map/while/body/eval_jaxpr/jit(_take)/gather | solution.py:73
  701.8 9.6 %reshape.292 = bf16[1536,2,5,128]{3,2,1,0:T(8,128)(2,1)} reshape(bf16[12,128,1280]{2,1,0:T(8,128)(2,1)} %gather_fusion) | data formatting | bytes 7864320 | tf_op jit(solution)/shard_map/while/body/eval_jaxpr/jit(_take)/gather | solution.py:73
  711.5 4.9 copy_select_fusion.2
  717.9 1.7 fusion.46
  722.1 10.5 %gather_fusion = bf16[12,128,1280]{2,1,0:T(8,128)(2,1)} fusion(bf16[72,128,1280]{2,1,0:T(8,128)(2,1)} %get-tuple-element.147, s32[1024]{0:T(1024)S(1)} %pad_clamp_fusion.3), kind=kCustom, calls=%fused_computation.clone.clone.1 | custom fusion | bytes 7864368 | tf_op jit(solution)/shard_map/while/body/eval_jaxpr/jit(_take)/gather | solution.py:73
  732.6 9.6 %reshape.292 = bf16[1536,2,5,128]{3,2,1,0:T(8,128)(2,1)} reshape(bf16[12,128,1280]{2,1,0:T(8,128)(2,1)} %gather_fusion) | data formatting | bytes 7864320 | tf_op jit(solution)/shard_map/while/body/eval_jaxpr/jit(_take)/gather | solution.py:73
  742.3 4.9 copy_select_fusion.2
  748.6 1.7 fusion.46
  752.8 10.5 %gather_fusion = bf16[12,128,1280]{2,1,0:T(8,128)(2,1)} fusion(bf16[72,128,1280]{2,1,0:T(8,128)(2,1)} %get-tuple-element.147, s32[1024]{0:T(1024)S(1)} %pad_clamp_fusion.3), kind=kCustom, calls=%fused_computation.clone.clone.1 | custom fusion | bytes 7864368 | tf_op jit(solution)/shard_map/while/body/eval_jaxpr/jit(_take)/gather | solution.py:73
  763.3 9.6 %reshape.292 = bf16[1536,2,5,128]{3,2,1,0:T(8,128)(2,1)} reshape(bf16[12,128,1280]{2,1,0:T(8,128)(2,1)} %gather_fusion) | data formatting | bytes 7864320 | tf_op jit(solution)/shard_map/while/body/eval_jaxpr/jit(_take)/gather | solution.py:73
  773.0 4.9 copy_select_fusion.2
  779.3 1.7 fusion.46
  783.5 10.5 %gather_fusion = bf16[12,128,1280]{2,1,0:T(8,128)(2,1)} fusion(bf16[72,128,1280]{2,1,0:T(8,128)(2,1)} %get-tuple-element.147, s32[1024]{0:T(1024)S(1)} %pad_clamp_fusion.3), kind=kCustom, calls=%fused_computation.clone.clone.1 | custom fusion | bytes 7864368 | tf_op jit(solution)/shard_map/while/body/eval_jaxpr/jit(_take)/gather | solution.py:73
  794.0 9.6 %reshape.292 = bf16[1536,2,5,128]{3,2,1,0:T(8,128)(2,1)} reshape(bf16[12,128,1280]{2,1,0:T(8,128)(2,1)} %gather_fusion) | data formatting | bytes 7864320 | tf_op jit(solution)/shard_map/while/body/eval_jaxpr/jit(_take)/gather | solution.py:73
  803.7 4.9 copy_select_fusion.2
  810.1 1.7 fusion.46
  814.2 10.5 %gather_fusion = bf16[12,128,1280]{2,1,0:T(8,128)(2,1)} fusion(bf16[72,128,1280]{2,1,0:T(8,128)(2,1)} %get-tuple-element.147, s32[1024]{0:T(1024)S(1)} %pad_clamp_fusion.3), kind=kCustom, calls=%fused_computation.clone.clone.1 | custom fusion | bytes 7864368 | tf_op jit(solution)/shard_map/while/body/eval_jaxpr/jit(_take)/gather | solution.py:73
  824.7 9.6 %reshape.292 = bf16[1536,2,5,128]{3,2,1,0:T(8,128)(2,1)} reshape(bf16[12,128,1280]{2,1,0:T(8,128)(2,1)} %gather_fusion) | data formatting | bytes 7864320 | tf_op jit(solution)/shard_map/while/body/eval_jaxpr/jit(_take)/gather | solution.py:73
  834.4 4.9 copy_select_fusion.2
  840.8 1.7 fusion.46
  845.0 10.5 %gather_fusion = bf16[12,128,1280]{2,1,0:T(8,128)(2,1)} fusion(bf16[72,128,1280]{2,1,0:T(8,128)(2,1)} %get-tuple-element.147, s32[1024]{0:T(1024)S(1)} %pad_clamp_fusion.3), kind=kCustom, calls=%fused_computation.clone.clone.1 | custom fusion | bytes 7864368 | tf_op jit(solution)/shard_map/while/body/eval_jaxpr/jit(_take)/gather | solution.py:73
  855.4 9.6 %reshape.292 = bf16[1536,2,5,128]{3,2,1,0:T(8,128)(2,1)} reshape(bf16[12,128,1280]{2,1,0:T(8,128)(2,1)} %gather_fusion) | data formatting | bytes 7864320 | tf_op jit(solution)/shard_map/while/body/eval_jaxpr/jit(_take)/gather | solution.py:73
  865.1 4.9 copy_select_fusion.2
  875.7 10.5 %gather_fusion = bf16[12,128,1280]{2,1,0:T(8,128)(2,1)} fusion(bf16[72,128,1280]{2,1,0:T(8,128)(2,1)} %get-tuple-element.147, s32[1024]{0:T(1024)S(1)} %pad_clamp_fusion.3), kind=kCustom, calls=%fused_computation.clone.clone.1 | custom fusion | bytes 7864368 | tf_op jit(solution)/shard_map/while/body/eval_jaxpr/jit(_take)/gather | solution.py:73
  886.2 9.6 %reshape.292 = bf16[1536,2,5,128]{3,2,1,0:T(8,128)(2,1)} reshape(bf16[12,128,1280]{2,1,0:T(8,128)(2,1)} %gather_fusion) | data formatting | bytes 7864320 | tf_op jit(solution)/shard_map/while/body/eval_jaxpr/jit(_take)/gather | solution.py:73
  895.9 4.9 copy_select_fusion.2
  906.4 23.6 %all_to_all.75 = bf16[8,128,640]{1,2,0:T(8,128)(2,1)S(1)} all-to-all(bf16[8,128,640]{1,2,0:T(8,128)(2,1)} %get-tuple-element.42), channel_id=1, replica_groups=mesh['seq'=32,'uly'=8] {'uly'}, dimensions={0} | all-to-all | bytes 2621440 | tf_op jit(solution)/shard_map/all_to_all | solution.py:84
  (123 shorter events, 44.4 us)
Async XLA Ops:
  0.0 23.9 %copy-start.3 = (bf16[128,5120]{1,0:T(8,128)(2,1)S(1)}, bf16[128,5120]{1,0:T(8,128)(2,1)}, u32[]{:S(2)}) copy-start(bf16[128,5120]{1,0:T(8,128)(2,1)} %param.9) | copy-start | bytes 3932164
  2.4 17.2 %all-to-all-start.2 = ((s32[32,1,8]{2,1,0:T(1,128)}), s32[32,1,8]{2,1,0:T(1,128)S(1)}, u32[]{:S(2)}, u32[]{:S(2)}) async-start(s32[32,1,8]{2,1,0:T(1,128)} %bitcast.4), calls=%async_computation.2 | async-start | bytes 32768 | tf_op jit(solution)/shard_map/all_to_all | solution.py:48
  19.6 23.0 %all-to-all-start = ((bf16[128,8,640]{0,2,1:T(8,128)(2,1)}), bf16[128,8,640]{0,2,1:T(8,128)(2,1)S(1)}, u32[]{:S(2)}, u32[]{:S(2)}) async-start(bf16[128,8,640]{0,2,1:T(8,128)(2,1)} %bitcast), calls=%async_computation | async-start | bytes 2621440 | tf_op jit(solution)/shard_map/all_to_all | solution.py:28
  42.7 22.3 %copy-start.1 = (bf16[128,8,640]{0,2,1:T(8,128)(2,1)}, bf16[128,8,640]{0,2,1:T(8,128)(2,1)S(1)}, u32[]{:S(2)}) copy-start(bf16[128,8,640]{0,2,1:T(8,128)(2,1)S(1)} %all-to-all-done) | copy-start | bytes 3932164
  42.7 22.2 %all-to-all-start.1 = ((bf16[128,8,640]{0,2,1:T(8,128)(2,1)}), bf16[128,8,640]{0,2,1:T(8,128)(2,1)S(1)}, u32[]{:S(2)}, u32[]{:S(2)}) async-start(bf16[128,8,640]{0,2,1:T(8,128)(2,1)} %bitcast.87), calls=%async_computation.1 | async-start | bytes 2621440 | tf_op jit(solution)/shard_map/all_to_all | solution.py:29
  64.9 1.1 copy-start.2
  94.4 504.9 %all-to-all-start.3 = ((bf16[32,2,128,1280]{2,3,1,0:T(8,128)(2,1)}), bf16[32,2,128,1280]{2,3,1,0:T(8,128)(2,1)}, u32[]{:S(2)}, u32[]{:S(2)}) async-start(bf16[32,2,128,1280]{2,3,1,0:T(8,128)(2,1)} %broadcast_select_fusion), calls=%async_computation.3 | async-start | bytes 41943040 | tf_op jit(solution)/shard_map/all_to_all | solution.py:58
  599.3 61.3 %all-to-all-start.4 = ((bf16[128,8,640]{0,2,1:T(8,128)(2,1)}), bf16[128,8,640]{0,2,1:T(8,128)(2,1)}, u32[]{:S(2)}, u32[]{:S(2)}) async-start(bf16[128,8,640]{0,2,1:T(8,128)(2,1)} %bitcast.88), calls=%async_computation.4 | async-start | bytes 2621440 | tf_op jit(solution)/shard_map/all_to_all | solution.py:27
  613.4 27.3 %copy-start = (bf16[8,128,1280]{2,1,0:T(8,128)(2,1)S(1)}, bf16[8,128,1280]{2,1,0:T(8,128)(2,1)}, u32[]{:S(2)}) copy-start(bf16[8,128,1280]{2,1,0:T(8,128)(2,1)} %copy.43) | copy-start | bytes 7864324
  640.8 19.8 %copy-start.4 = (s32[8]{0:T(128)S(1)}, s32[8]{0:T(128)}, u32[]{:S(2)}) copy-start(s32[8]{0:T(128)} %param.11) | copy-start | bytes 100
where the time goes:
time: 935 us; the launch traced here: 931 us
  waiting for transfers between devices  531 us (57%)
  local copies, waits for them, and re-layouts  222 us (24%)
  other arithmetic  92 us (10%)
  starting transfers between devices  40.4 us (4%)
  blocking collectives  23.6 us (3%)
  matrix products  22.4 us (2%)
    all_to_all x1, waiting for transfers between devices, body(): lax.all_to_all(outgoing, 'seq', split_axis=0, concat_axis=0, tiled=True)  491 us
    gather x16, local copies, waits for them, and re-layouts, attend(): jnp.take(pool, slot_list, axis=0)  161 us
    select_n x16, other arithmetic, attend(): jnp.take(pool, slot_list, axis=0)  39.6 us
    all_to_all x1, local copies, waits for them, and re-layouts, body(): lax.all_to_all(outgoing, 'seq', split_axis=0, concat_axis=0, tiled=True)  27.3 us
    all_to_all x1, blocking collectives, body(): lax.all_to_all(attended.reshape(row_count, feat_width), 'uly', split_axis...  23.6 us
    concatenate x1, other arithmetic, body(): jnp.concatenate([kv_pairs, arrived.reshape(groups * PEER_SLOTS, BLOCK_LEN...  19.8 us
  transfers between devices with their start and end apart: 5, of which 4 were waited for; matrix products, arithmetic and copies ran while one was open for 6% of the time, Pallas kernels for 0%

commit v1 on v0

v1 whole, which is shorter than its diff:
```python
import jax
import jax.numpy as jnp
from jax import lax
from jax.experimental import pallas as pl
from jax.experimental.pallas import tpu as pltpu
from jax.sharding import PartitionSpec as P

NZ, NY, NX, NC = 8, 4, 4, 2
HD = 128
BL = 128
LIST_LEN = 12
NBLOCKS = NZ * NY * NX * NC
PLANE_HEADS = NX + 1
MESH = pl.DeviceIdType.MESH
EXP2_SCALE = HD ** (-0.5) * 1.4426950408889634
ORDER = (0, 1, 7, 2, 6, 3, 5, 4)
SLOT_B_LANE = 16
COUNT_LANE = 32


def rem(a, n):
    return lax.rem(a, jnp.int32(n))


def div(a, n):
    return lax.div(a, jnp.int32(n))


def kernel(q_ref, k_ref, v_ref, meta_ref, out_ref, kv, qv, ov, meta_v, meta_s, s_ref, l_kv, l_q, l_m, l_o, l_s,
           s_1, s_m, s_a, s_b, s_o, r_a1, r_b1, r_q, r_m, r_o, r_ay, r_ay2, r_as, r_by, r_by2, r_bs, r_bx, r_bxh, r_bx2):
    s = lax.axis_index("seq")
    u = lax.axis_index("uly")
    z, y = div(s, NY), rem(s, NY)
    x, c = div(u, NC), rem(u, NC)

    def dev(z2, y2, x2, c2):
        return (z2 * NY + y2, x2 * NC + c2)

    yp, ym = rem(y + 1, NY), rem(y + NY - 1, NY)
    y2 = rem(y + 2, NY)
    xp, xm = rem(x + 1, NX), rem(x + NX - 1, NX)
    x2 = rem(x + 2, NX)
    sib = dev(z, y, x, 1 - c)
    y_plus, y_minus = dev(z, yp, x, c), dev(z, ym, x, c)
    x_plus, x_minus = dev(z, y, xp, c), dev(z, y, xm, c)

    def slot_a(zz, yy, xx, cc):
        return ((yy * NC + cc) * NZ + zz) * NX + xx

    def base_b(xx, cc, yy):
        return NBLOCKS + ((xx * NC + cc) * NY + yy) * NZ

    def cols(h):
        return pl.ds(pl.multiple_of(h * HD, HD), HD)

    def wait(ref, sem):
        pltpu.make_async_copy(ref, ref, sem).wait()

    def local(src, dst, sem):
        pltpu.make_async_copy(src, dst, sem).start()

    def remote(src, dst, send, recv, target):
        pltpu.make_async_remote_copy(
            src_ref=src, dst_ref=dst, send_sem=send, recv_sem=recv, device_id=target, device_id_type=MESH
        ).start()

    me_a = slot_a(z, y, x, c)
    me_b = base_b(x, c, y) + z
    head_a, head_b = PLANE_HEADS * z + x, PLANE_HEADS * z + NX
    local(meta_ref, meta_v.at[z], l_m)
    local(k_ref.at[:, cols(head_b)], kv.at[me_b, 0], l_kv.at[1])
    local(v_ref.at[:, cols(head_b)], kv.at[me_b, 1], l_kv.at[1])
    local(k_ref.at[:, cols(head_a)], kv.at[me_a, 0], l_kv.at[0])
    local(v_ref.at[:, cols(head_a)], kv.at[me_a, 1], l_kv.at[0])
    local(q_ref.at[:, cols(head_a)], qv.at[z * NX + x], l_q)
    local(q_ref.at[:, cols(head_b)], qv.at[NZ * NX + z], l_q)

    barrier = pltpu.get_barrier_semaphore()

    def greet(i, carry):
        zz, xx = rem(z + div(i, NX), NZ), rem(x + rem(i, NX), NX)
        pl.semaphore_signal(barrier, inc=1, device_id=dev(zz, y, xx, c), device_id_type=MESH)
        return carry

    lax.fori_loop(1, NZ * NX, greet, 0)
    for target in (sib, y_plus, y_minus):
        pl.semaphore_signal(barrier, inc=1, device_id=target, device_id_type=MESH)
    pl.semaphore_wait(barrier, NZ * NX - 1 + 3)

    def step_to(j):
        half = div(j + 1, 2)
        return jnp.where(rem(j, 2) == 1, half, NZ - half)

    def send_meta_b(j, carry):
        t = step_to(j)
        zz = rem(z + t, NZ)
        target = dev(zz, y, x, c)
        h = PLANE_HEADS * zz + NX
        remote(meta_ref, meta_v.at[z], s_m, r_m, target)
        remote(k_ref.at[:, cols(h)], kv.at[me_b, 0], s_1, r_b1, target)
        remote(v_ref.at[:, cols(h)], kv.at[me_b, 1], s_1, r_b1, target)
        return carry

    lax.fori_loop(1, NZ, send_meta_b, 0)

    def send_a(i, carry):
        j = div(i, NX)
        t = jnp.where(j == 0, 0, step_to(j))
        zz, xx = rem(z + t, NZ), rem(x + rem(i, NX), NX)
        target = dev(zz, y, xx, c)
        h = PLANE_HEADS * zz + xx
        o = rem(NZ - t, NZ)
        remote(k_ref.at[:, cols(h)], kv.at[me_a, 0], s_1, r_a1.at[o], target)
        remote(v_ref.at[:, cols(h)], kv.at[me_a, 1], s_1, r_a1.at[o], target)
        return carry

    lax.fori_loop(1, NZ * NX, send_a, 0)

    def send_q(i, carry):
        j = div(i, NX)
        t = jnp.where(j == 0, 0, step_to(j))
        zz, xx = rem(z + t, NZ), rem(x + rem(i, NX), NX)
        remote(q_ref.at[:, cols(PLANE_HEADS * zz + xx)], qv.at[z * NX + x], s_1, r_q, dev(zz, y, xx, c))
        return carry

    lax.fori_loop(1, NZ * NX, send_q, 0)

    def send_qb(j, carry):
        zz = rem(z + step_to(j), NZ)
        remote(q_ref.at[:, cols(PLANE_HEADS * zz + NX)], qv.at[NZ * NX + z], s_1, r_q, dev(zz, y, x, c))
        return carry

    lax.fori_loop(1, NZ, send_qb, 0)

    sent = {"a": 0, "b": 0}

    def push(which, start, n, recv, target):
        part = kv.at[pl.ds(start, n)]
        sent[which] += n
        remote(part, part, s_a if which == "a" else s_b, recv, target)

    def a_own(o):
        base = slot_a(rem(z + o, NZ), y, 0, c)
        if o == 0:
            wait(kv.at[pl.ds(base, NX - 1)], r_a1.at[0])
            wait(kv.at[me_a], l_kv.at[0])
        else:
            wait(kv.at[pl.ds(base, NX)], r_a1.at[o])
        push("a", base, NX, r_ay.at[0, o], y_plus)
        push("a", base, NX, r_ay.at[1, o], y_minus)
        push("a", base, NX, r_as, sib)

    def a_from(side, o):
        base = slot_a(rem(z + o, NZ), ym if side == 0 else yp, 0, c)
        wait(kv.at[pl.ds(base, NX)], r_ay.at[side, o])
        if (o < NZ // 2) == (side == 0):
            push("a", base, NX, r_ay2.at[o], y_plus if side == 0 else y_minus)
        push("a", base, NX, r_as, sib)

    def a_far(o):
        base = slot_a(rem(z + o, NZ), y2, 0, c)
        wait(kv.at[pl.ds(base, NX)], r_ay2.at[o])
        push("a", base, NX, r_as, sib)

    half_z = NZ // 2
    b_rows = (y, ym, yp)

    def b_spread(row, start, n, sems):
        push("b", start, n, sems[0], x_plus)
        push("b", start, n, sems[1], x_minus)
        push("b", start, n, r_bs, sib)

    def b_own():
        base = base_b(x, c, y)
        wait(kv.at[pl.ds(base, NZ - 1)], r_b1)
        wait(kv.at[me_b], l_kv.at[1])
        push("b", base, NZ, r_by.at[0], y_plus)
        push("b", base, NZ, r_by.at[1], y_minus)
        b_spread(0, base, NZ, (r_bx.at[0, 0], r_bx.at[1, 0]))

    def b_from(side):
        base = base_b(x, c, ym if side == 0 else yp)
        wait(kv.at[pl.ds(base, NZ)], r_by.at[side])
        if side == 0:
            push("b", base, half_z, r_by2.at[0], y_plus)
        else:
            push("b", base + half_z, half_z, r_by2.at[1], y_minus)
        b_spread(1 + side, base, NZ, (r_bx.at[0, 1 + side], r_bx.at[1, 1 + side]))

    def b_far(part):
        base = base_b(x, c, y2) + part * half_z
        wait(kv.at[pl.ds(base, half_z)], r_by2.at[part])
        b_spread(3, base, half_z, (r_bxh.at[0, part], r_bxh.at[1, part]))

    def bx_from(side, row):
        base = base_b(xm if side == 0 else xp, c, b_rows[row])
        wait(kv.at[pl.ds(base, NZ)], r_bx.at[side, row])
        part = base + side * half_z
        push("b", part, half_z, r_bx2.at[side, row], x_plus if side == 0 else x_minus)
        push("b", base, NZ, r_bs, sib)

    def bx_half(side, part):
        base = base_b(xm if side == 0 else xp, c, y2) + part * half_z
        wait(kv.at[pl.ds(base, half_z)], r_bxh.at[side, part])
        if side == part:
            push("b", base, half_z, r_bx2.at[side, 3], x_plus if side == 0 else x_minus)
        push("b", base, half_z, r_bs, sib)

    def bx_far(side, row):
        yy = y2 if row == 3 else b_rows[row]
        base = base_b(x2, c, yy) + side * half_z
        wait(kv.at[pl.ds(base, half_z)], r_bx2.at[side, row])
        push("b", base, half_z, r_bs, sib)

    b_own()
    a_own(0)
    b_from(0)
    b_from(1)
    a_own(1)
    a_own(7)
    b_far(0)
    b_far(1)
    for side in (0, 1):
        a_from(side, 0)
        bx_from(side, 0)
    a_own(2)
    a_own(6)
    for o in (1, 7):
        a_from(0, o)
        a_from(1, o)
    a_own(3)
    a_own(5)
    for side in (0, 1):
        bx_from(side, 1)
    a_own(4)
    for o in (2, 6):
        a_from(0, o)
        a_from(1, o)
    for side in (0, 1):
        bx_from(side, 2)
    for o in (3, 5, 4):
        a_from(0, o)
        a_from(1, o)
    for side in (0, 1):
        for part in (0, 1):
            bx_half(side, part)
    for o in ORDER:
        a_far(o)
    for row in range(4):
        bx_far(0, row)
        bx_far(1, row)

    wait(meta_v.at[0], l_m)
    wait(meta_v.at[pl.ds(0, NZ - 1)], r_m)
    to_smem = pltpu.make_async_copy(meta_v, meta_s, l_s)
    to_smem.start()
    to_smem.wait()
    units = NZ * NX + NZ
    wait(qv.at[pl.ds(0, 2)], l_q)
    wait(qv.at[pl.ds(0, units - 2)], r_q)
    wait(kv.at[pl.ds(0, NBLOCKS // 2)], r_as)
    wait(kv.at[pl.ds(0, NBLOCKS // 2)], r_bs)

    key_ids = lax.broadcasted_iota(jnp.int32, (BL, 2 * BL), 1)

    def place(t):
        is_b = t >= NZ * NX
        i = jnp.where(is_b, t - NZ * NX, div(t, NX))
        far = jnp.where(rem(i, 2) == 1, NZ - div(i + 1, 2), div(i, 2))
        zz = rem(z + NZ // 2 + far, NZ)
        xx = jnp.where(is_b, x, rem(x + rem(t, NX), NX))
        unit = jnp.where(is_b, NZ * NX + zz, zz * NX + xx)
        return is_b, zz, xx, unit

    def attend(t):
        is_b, zz, xx, unit = place(t)
        row = xx * NC + c
        lane = jnp.where(is_b, SLOT_B_LANE, 0)
        count = meta_s[zz, row, COUNT_LANE]
        slots = [meta_s[zz, row, lane + e] for e in range(LIST_LEN)]
        q = qv[unit]
        top = None
        for p in range(LIST_LEN // 2):
            keys = jnp.concatenate([kv[slots[2 * p], 0], kv[slots[2 * p + 1], 0]], axis=0)
            scores = lax.dot_general(q, keys, (((1,), (1,)), ((), ())), preferred_element_type=jnp.float32)
            if p >= 2:
                scores = jnp.where(key_ids < (count - 2 * p) * BL, scores, -jnp.inf)
            s_ref[p] = scores
            top = scores if top is None else jnp.maximum(top, scores)
        row_max = jnp.max(top, axis=1, keepdims=True)
        total = None
        blended = None
        for p in range(LIST_LEN // 2):
            weights = jnp.exp2((s_ref[p] - row_max) * EXP2_SCALE)
            vals = jnp.concatenate([kv[slots[2 * p], 1], kv[slots[2 * p + 1], 1]], axis=0)
            part = jnp.dot(weights.astype(jnp.bfloat16), vals, preferred_element_type=jnp.float32)
            blended = part if blended is None else blended + part
            total = weights if total is None else total + weights
        weight_sum = jnp.sum(total, axis=1, keepdims=True)
        ov[unit] = (blended / weight_sum).astype(jnp.bfloat16)

    def give(t):
        is_b, zz, xx, unit = place(t)
        dst = out_ref.at[:, cols(jnp.where(is_b, head_b, head_a))]
        mine = (zz == z) & (xx == x)

        @pl.when(mine)
        def _():
            local(ov.at[unit], dst, l_o)

        @pl.when(jnp.logical_not(mine))
        def _():
            remote(ov.at[unit], dst, s_o, r_o, dev(zz, y, xx, c))

    def work(t, carry):
        attend(t)

        @pl.when(t > 0)
        def _():
            give(t - 1)

        return carry

    lax.fori_loop(0, units, work, 0)
    give(jnp.int32(units - 1))

    wait(qv.at[pl.ds(0, units - 2)], r_o)
    wait(qv.at[pl.ds(0, 2)], l_o)
    wait(qv.at[pl.ds(0, units - 2)], s_o)
    wait(meta_v.at[pl.ds(0, NZ - 1)], s_m)
    wait(kv.at[pl.ds(0, (units - 2) * 3 // 2)], s_1)
    wait(kv.at[pl.ds(0, sent["a"])], s_a)
    wait(kv.at[pl.ds(0, sent["b"])], s_b)


def body(queries, keys, values, block_lists, block_counts):
    zz, rest = block_lists // (NY * NX * NC), block_lists % (NY * NX * NC)
    yy, rest = rest // (NX * NC), rest % (NX * NC)
    xx, cc = rest // NC, rest % NC
    slot_a = ((yy * NC + cc) * NZ + zz) * NX + xx
    slot_b = NBLOCKS + ((xx * NC + cc) * NY + yy) * NZ + zz
    rows = block_lists.shape[0]
    gap = jnp.zeros((rows, SLOT_B_LANE - LIST_LEN), jnp.int32)
    meta = jnp.concatenate(
        [slot_a, gap, slot_b, gap, block_counts[:, None], jnp.zeros((rows, 128 - COUNT_LANE - 1), jnp.int32)], axis=1
    )
    dma = pltpu.SemaphoreType.DMA
    units = NZ * NX + NZ
    return pl.pallas_call(
        kernel,
        out_shape=jax.ShapeDtypeStruct(queries.shape, jnp.bfloat16),
        in_specs=[pl.BlockSpec(memory_space=pl.ANY)] * 4,
        out_specs=pl.BlockSpec(memory_space=pl.ANY),
        scratch_shapes=[
            pltpu.VMEM((2 * NBLOCKS, 2, BL, HD), jnp.bfloat16),
            pltpu.VMEM((units, BL, HD), jnp.bfloat16),
            pltpu.VMEM((units, BL, HD), jnp.bfloat16),
            pltpu.VMEM((NZ, NX * NC, 128), jnp.int32),
            pltpu.SMEM((NZ, NX * NC, 128), jnp.int32),
            pltpu.VMEM((LIST_LEN // 2, BL, 2 * BL), jnp.float32),
            dma((2,)), dma, dma, dma, dma,
            dma, dma, dma, dma, dma,
            dma((NZ,)), dma, dma, dma, dma,
            dma((2, NZ)), dma((NZ,)), dma,
            dma((2,)), dma((2,)), dma, dma((2, 3)), dma((2, 2)), dma((2, 4)),
        ],
        compiler_params=pltpu.CompilerParams(collective_id=0, has_side_effects=True, vmem_limit_bytes=52 << 20),
    )(queries, keys, values, meta)


def solution(mesh):
    placed = (
        P(("seq", "uly"), None),
        P(("seq", "uly"), None),
        P(("seq", "uly"), None),
        P("seq", None),
        P("seq"),
    )
    return jax.shard_map(
        body, mesh=mesh, in_specs=placed, out_specs=P(("seq", "uly"), None), check_vma=False
    )
```

time: 935 us -> 159 us (0.17)
  the two profiles are of different devices: /device:TPU:96 before, /device:TPU:1 now
where the time goes in v1:
time: 159 us
  Pallas kernels  156 us (98%)
  local copies, waits for them, and re-layouts  1.87 us (1%)
    pallas_call x1, Pallas kernels, body(): pl.pallas_call(kernel, out_shape=jax.ShapeDtypeStruct(queries.shape, jnp....  156 us

profile of v1, /device:TPU:1, one launch (start us, length us, event | category | flops | bytes accessed | tf_op | source)
XLA Modules:
  0.0 159.0 jit_solution(2274561734326872258)
XLA Ops:
  0.0 0.7 copy.6
  0.7 0.7 add_add_fusion
  1.5 0.1 concatenate.3.meta_ref
  1.5 156.4 %shard_map.55 = bf16[128,5120]{1,0:T(8,128)(2,1)S(1)} custom-call(bf16[128,5120]{1,0:T(8,128)(2,1)} %q_ref.1, bf16[128,5120]{1,0:T(8,128)(2,1)} %k_ref.1, bf16[128,5120]{1,0:T(8,128)(2,1)} %v_ref.1, s32[8,128]{1,0:T(8,128)S(1)} %concatenate.3.meta_ref), custom_call_target="tpu_custom_call" | custom-call | tf_op jit(solution)/shard_map/pallas_call | solution.py:349
  158.0 1.1 copy.8
  (2 shorter events, 0.0 us)

commit v2 on v1

v2 whole, which is shorter than its diff:
```python
import jax
import jax.numpy as jnp
from jax import lax
from jax.experimental import pallas as pl
from jax.experimental.pallas import tpu as pltpu
from jax.sharding import PartitionSpec as P

NZ, NY, NX, NC = 8, 4, 4, 2
HD = 128
BL = 128
LIST_LEN = 12
NBLOCKS = NZ * NY * NX * NC
PLANE_HEADS = NX + 1
MESH = pl.DeviceIdType.MESH
EXP2_SCALE = HD ** (-0.5) * 1.4426950408889634
ORDER = (0, 1, 7, 2, 6, 3, 5, 4)
NEAR = 2
LAST = (NZ - 1) * NX // 2
SLOT_B_LANE = 16
COUNT_LANE = 32


def rem(a, n):
    return lax.rem(a, jnp.int32(n))


def div(a, n):
    return lax.div(a, jnp.int32(n))


def kernel(q_ref, k_ref, v_ref, meta_ref, out_ref, kva, kvb, qv, ov, meta_v, meta_s, s_ref, l_kv, l_q, l_m, l_o, l_s,
           s_1, s_q, s_m, s_a, s_b, s_o, r_a1, r_b1, r_q, r_qb, r_m, r_o, r_ay, r_ay2, r_as, r_by, r_by2, r_bs, r_bx, r_bxh, r_bx2,
           r_cx, r_cx2, r_cy, r_cy2):
    s = lax.axis_index("seq")
    u = lax.axis_index("uly")
    z, y = div(s, NY), rem(s, NY)
    x, c = div(u, NC), rem(u, NC)

    def dev(z2, y2, x2, c2):
        return (z2 * NY + y2, x2 * NC + c2)

    yp, ym = rem(y + 1, NY), rem(y + NY - 1, NY)
    y2 = rem(y + 2, NY)
    xp, xm = rem(x + 1, NX), rem(x + NX - 1, NX)
    x2 = rem(x + 2, NX)
    sib = dev(z, y, x, 1 - c)
    y_plus, y_minus = dev(z, yp, x, c), dev(z, ym, x, c)
    x_plus, x_minus = dev(z, y, xp, c), dev(z, y, xm, c)

    def slot_a(zz, yy, xx, cc):
        return ((yy * NC + cc) * NZ + zz) * NX + xx

    def base_b(xx, cc, yy):
        return ((xx * NC + cc) * NY + yy) * NZ

    def place_of(o):
        return jnp.where(o <= NZ // 2, jnp.maximum(2 * o - 1, 0), 2 * (NZ - o))

    def cols(h):
        return pl.ds(pl.multiple_of(h * HD, HD), HD)

    def wait(ref, sem):
        pltpu.make_async_copy(ref, ref, sem).wait()

    def local(src, dst, sem):
        pltpu.make_async_copy(src, dst, sem).start()

    def remote(src, dst, send, recv, target):
        pltpu.make_async_remote_copy(
            src_ref=src, dst_ref=dst, send_sem=send, recv_sem=recv, device_id=target, device_id_type=MESH
        ).start()

    me_a = slot_a(z, y, x, c)
    me_b = base_b(x, c, y)
    head_a, head_b = PLANE_HEADS * z + x, PLANE_HEADS * z + NX
    local(meta_ref, meta_v.at[z], l_m)
    local(k_ref.at[:, cols(head_b)], kvb.at[me_b, 0], l_kv.at[1])
    local(v_ref.at[:, cols(head_b)], kvb.at[me_b, 1], l_kv.at[1])
    local(k_ref.at[:, cols(head_a)], kva.at[me_a, 0], l_kv.at[0])
    local(v_ref.at[:, cols(head_a)], kva.at[me_a, 1], l_kv.at[0])
    local(q_ref.at[:, cols(head_a)], qv.at[z * NX + x], l_q.at[0])
    local(q_ref.at[:, cols(head_b)], qv.at[NZ * NX + z], l_q.at[1])

    barrier = pltpu.get_barrier_semaphore()

    def greet(i, carry):
        zz, xx = rem(z + div(i, NX), NZ), rem(x + rem(i, NX), NX)
        pl.semaphore_signal(barrier, inc=1, device_id=dev(zz, y, xx, c), device_id_type=MESH)
        return carry

    lax.fori_loop(1, NZ * NX, greet, 0)
    for target in (sib, y_plus, y_minus):
        pl.semaphore_signal(barrier, inc=1, device_id=target, device_id_type=MESH)
    pl.semaphore_wait(barrier, NZ * NX - 1 + 3)

    sent = {"a": 0, "b": 0}

    def push(which, start, n, recv, target):
        part = (kva if which == "a" else kvb).at[pl.ds(start, n)]
        sent[which] += n
        remote(part, part, s_a if which == "a" else s_b, recv, target)

    def a_one(at):
        push("a", at, 1, r_ay.at[0, 0], y_plus)
        push("a", at, 1, r_ay.at[1, 0], y_minus)
        push("a", at, 1, r_as, sib)

    def a_own(o):
        base = slot_a(rem(z + o, NZ), y, 0, c)
        if o == 0:
            wait(kva.at[pl.ds(base, NX - 1)], r_a1.at[0])
            for r in range(1, NX):
                a_one(slot_a(z, y, rem(x + r, NX), c))
            return
        wait(kva.at[pl.ds(base, NX)], r_a1.at[o])
        push("a", base, NX, r_ay.at[0, o], y_plus)
        push("a", base, NX, r_ay.at[1, o], y_minus)
        push("a", base, NX, r_as, sib)

    def a_from(side, o):
        base = slot_a(rem(z + o, NZ), ym if side == 0 else yp, 0, c)
        wait(kva.at[pl.ds(base, NX)], r_ay.at[side, o])
        if (o < NZ // 2) == (side == 0):
            push("a", base, NX, r_ay2.at[o], y_plus if side == 0 else y_minus)
        push("a", base, NX, r_as, sib)

    def a_far(o):
        base = slot_a(rem(z + o, NZ), y2, 0, c)
        wait(kva.at[pl.ds(base, NX)], r_ay2.at[o])
        push("a", base, NX, r_as, sib)

    near, rest = NEAR, NZ - NEAR
    half_n, half_r = near // 2, rest // 2
    b_rows = (y, ym, yp, y2)
    b_cols = (x, xm, xp, x2)

    def b_row(p):
        push("b", base_b(x, c, y) + p, 1, r_cy.at[0, 0], y_plus)
        push("b", base_b(x, c, y) + p, 1, r_cy.at[1, 0], y_minus)

    def b_own(p):
        base = base_b(x, c, y)
        if p == 0:
            wait(kvb.at[base], l_kv.at[1])
        else:
            wait(kvb.at[base + p], r_b1.at[p])
        if p < near:
            push("b", base + p, 1, r_cx.at[0], x_plus)
            push("b", base + p, 1, r_cx.at[1], x_minus)
            if p == 0:
                b_row(p)
        else:
            push("b", base + p, 1, r_by.at[0], y_plus)
            push("b", base + p, 1, r_by.at[1], y_minus)
            push("b", base + p, 1, r_bx.at[0, 0], x_plus)
            push("b", base + p, 1, r_bx.at[1, 0], x_minus)
        push("b", base + p, 1, r_bs, sib)

    def b_from(side):
        base = base_b(x, c, b_rows[1 + side]) + near
        wait(kvb.at[pl.ds(base, rest)], r_by.at[side])
        push("b", base + side * half_r, half_r, r_by2.at[side], y_minus if side else y_plus)
        push("b", base, rest, r_bx.at[0, 1 + side], x_plus)
        push("b", base, rest, r_bx.at[1, 1 + side], x_minus)
        push("b", base, rest, r_bs, sib)

    def b_far(part):
        base = base_b(x, c, y2) + near + part * half_r
        wait(kvb.at[pl.ds(base, half_r)], r_by2.at[part])
        push("b", base, half_r, r_bxh.at[0, part], x_plus)
        push("b", base, half_r, r_bxh.at[1, part], x_minus)
        push("b", base, half_r, r_bs, sib)

    def bx_from(side, row):
        base = base_b(b_cols[1 + side], c, b_rows[row]) + near
        wait(kvb.at[pl.ds(base, rest)], r_bx.at[side, row])
        push("b", base + side * half_r, half_r, r_bx2.at[side, row], x_minus if side else x_plus)
        push("b", base, rest, r_bs, sib)

    def bx_half(side, part):
        base = base_b(b_cols[1 + side], c, y2) + near + part * half_r
        wait(kvb.at[pl.ds(base, half_r)], r_bxh.at[side, part])
        if side == part:
            push("b", base, half_r, r_bx2.at[side, 3], x_minus if side else x_plus)
        push("b", base, half_r, r_bs, sib)

    def bx_far(side, row):
        base = base_b(x2, c, b_rows[row]) + near + side * half_r
        wait(kvb.at[pl.ds(base, half_r)], r_bx2.at[side, row])
        push("b", base, half_r, r_bs, sib)

    def c_from(side):
        base = base_b(b_cols[1 + side], c, y)
        wait(kvb.at[pl.ds(base, near)], r_cx.at[side])
        push("b", base + side * half_n, half_n, r_cx2.at[side], x_minus if side else x_plus)
        push("b", base, near, r_bs, sib)

    def c_far(part):
        base = base_b(x2, c, y) + part * half_n
        wait(kvb.at[pl.ds(base, half_n)], r_cx2.at[part])
        push("b", base, half_n, r_bs, sib)

    def c_spread(col):
        base = base_b(b_cols[col], c, y)
        push("b", base, near, r_cy.at[0, col], y_plus)
        push("b", base, near, r_cy.at[1, col], y_minus)

    def cy_from(side, col):
        base = base_b(b_cols[col], c, b_rows[1 + side])
        wait(kvb.at[pl.ds(base, near)], r_cy.at[side, col])
        push("b", base + side * half_n, half_n, r_cy2.at[side, col], y_minus if side else y_plus)
        push("b", base, near, r_bs, sib)

    def cy_far(side, col):
        base = base_b(b_cols[col], c, y2) + side * half_n
        wait(kvb.at[pl.ds(base, half_n)], r_cy2.at[side, col])
        push("b", base, half_n, r_bs, sib)

    wait(kva.at[me_a], l_kv.at[0])
    a_one(me_a)
    b_own(0)

    def step_to(j):
        half = div(j + 1, 2)
        return jnp.where(rem(j, 2) == 1, half, NZ - half)

    def send_meta_b(j, carry):
        t = step_to(j)
        zz = rem(z + t, NZ)
        target = dev(zz, y, x, c)
        h = PLANE_HEADS * zz + NX
        remote(meta_ref, meta_v.at[z], s_m, r_m, target)
        there = me_b + place_of(NZ - t)
        remote(k_ref.at[:, cols(h)], kvb.at[there, 0], s_1, r_b1.at[place_of(NZ - t)], target)
        remote(v_ref.at[:, cols(h)], kvb.at[there, 1], s_1, r_b1.at[place_of(NZ - t)], target)
        return carry

    lax.fori_loop(1, NZ, send_meta_b, 0)

    def send_a(i, carry):
        j = div(i, NX)
        t = jnp.where(j == 0, 0, step_to(j))
        zz, xx = rem(z + t, NZ), rem(x + rem(i, NX), NX)
        target = dev(zz, y, xx, c)
        h = PLANE_HEADS * zz + xx
        o = rem(NZ - t, NZ)
        remote(k_ref.at[:, cols(h)], kva.at[me_a, 0], s_1, r_a1.at[o], target)
        remote(v_ref.at[:, cols(h)], kva.at[me_a, 1], s_1, r_a1.at[o], target)
        return carry

    lax.fori_loop(1, NZ * NX, send_a, 0)

    def send_q(i, carry):
        j = div(i, NX)
        t = jnp.where(j == 0, 0, step_to(j))
        zz, xx = rem(z + t, NZ), rem(x + rem(i, NX), NX)
        remote(q_ref.at[:, cols(PLANE_HEADS * zz + xx)], qv.at[z * NX + x], s_q, r_q.at[rem(NZ - t, NZ)], dev(zz, y, xx, c))
        return carry

    lax.fori_loop(1, NZ * NX, send_q, 0)

    def send_qb(j, carry):
        zz = rem(z + step_to(j), NZ)
        remote(q_ref.at[:, cols(PLANE_HEADS * zz + NX)], qv.at[NZ * NX + z], s_q, r_qb, dev(zz, y, x, c))
        return carry

    lax.fori_loop(1, NZ, send_qb, 0)

    def both(f, *args):
        for side in (0, 1):
            f(side, *args)

    b_own(1)
    a_own(0)
    for p in range(2, NZ):
        b_own(p)
    a_own(1)
    a_own(7)
    both(b_from)
    both(c_from)
    both(a_from, 0)
    a_own(2)
    both(bx_from, 0)
    a_own(6)
    both(a_from, 1)
    both(b_far)
    both(a_from, 7)
    a_own(3)
    both(bx_from, 1)
    a_own(5)
    both(a_from, 2)
    both(a_from, 6)
    a_own(4)
    for o in (0, 1, 7):
        a_far(o)
    both(a_from, 3)
    both(c_far)
    both(bx_from, 2)
    both(a_from, 5)
    for o in (2, 6):
        a_far(o)
    both(a_from, 4)
    b_row(1)
    for col in (1, 2, 3):
        c_spread(col)
    both(bx_half, 0)
    both(bx_half, 1)
    for o in (3, 5, 4):
        a_far(o)

    wait(meta_v.at[0], l_m)
    wait(meta_v.at[pl.ds(0, NZ - 1)], r_m)
    to_smem = pltpu.make_async_copy(meta_v, meta_s, l_s)
    to_smem.start()
    to_smem.wait()
    wait(kva.at[pl.ds(0, NBLOCKS // 2)], r_as)

    key_ids = lax.broadcasted_iota(jnp.int32, (BL, 2 * BL), 1)

    def weigh(kv, part, row, lane, zz, unit):
        count = meta_s[zz, row, COUNT_LANE]
        slots = [meta_s[zz, row, lane + e] for e in range(LIST_LEN)]
        if lane:
            slots = [n // NZ * NZ + place_of(rem(n % NZ + NZ - z, NZ)) for n in slots]
        q = qv[unit]
        top = None
        for p in range(LIST_LEN // 2):
            keys = jnp.concatenate([kv[slots[2 * p], 0], kv[slots[2 * p + 1], 0]], axis=0)
            scores = lax.dot_general(q, keys, (((1,), (1,)), ((), ())), preferred_element_type=jnp.float32)
            if p >= 2:
                scores = jnp.where(key_ids < (count - 2 * p) * BL, scores, -jnp.inf)
            s_ref[part, p] = scores
            top = scores if top is None else jnp.maximum(top, scores)
        return slots, jnp.max(top, axis=1, keepdims=True)

    def blend(kv, part, unit, slots, row_max):
        total = None
        blended = None
        for p in range(LIST_LEN // 2):
            weights = jnp.exp2((s_ref[part, p] - row_max) * EXP2_SCALE)
            vals = jnp.concatenate([kv[slots[2 * p], 1], kv[slots[2 * p + 1], 1]], axis=0)
            piece = jnp.dot(weights.astype(jnp.bfloat16), vals, preferred_element_type=jnp.float32)
            blended = piece if blended is None else blended + piece
            total = weights if total is None else total + weights
        weight_sum = jnp.sum(total, axis=1, keepdims=True)
        ov[unit] = (blended / weight_sum).astype(jnp.bfloat16)

    def attend(kv, lane, picks):
        state = [weigh(kv, n, row, lane, zz, unit) for n, (row, zz, unit) in enumerate(picks)]
        for n, (row, zz, unit) in enumerate(picks):
            blend(kv, n, unit, *state[n])

    def give(zz, xx, unit, head):
        dst = out_ref.at[:, cols(head)]
        mine = (zz == z) & (xx == x)

        @pl.when(mine)
        def _():
            local(ov.at[unit], dst, l_o)

        @pl.when(jnp.logical_not(mine))
        def _():
            remote(ov.at[unit], dst, s_o, r_o, dev(zz, y, xx, c))

    def turn(g):
        return jnp.where(rem(g, 2) == 1, NZ // 2 - div(g + 1, 2), NZ // 2 + div(g, 2))

    def give_a(t):
        zz = rem(z + turn(div(t, NX)), NZ)
        xx = rem(x + rem(t, NX), NX)
        give(zz, xx, zz * NX + xx, head_a)

    def give_b(t):
        zz = rem(z + turn(t), NZ)
        give(zz, x, NZ * NX + zz, head_b)

    def work_a(i, carry):
        picks = []
        for t in (2 * i, 2 * i + 1):
            zz = rem(z + turn(div(t, NX)), NZ)
            xx = rem(x + rem(t, NX), NX)
            picks.append((xx * NC + c, zz, zz * NX + xx))
        attend(kva, 0, picks)

        @pl.when((i > 0) & (i != LAST))
        def _():
            give_a(2 * i - 2)
            give_a(2 * i - 1)

        return carry

    def work_b(i, carry):
        picks = []
        for t in (2 * i, 2 * i + 1):
            zz = rem(z + turn(t), NZ)
            picks.append((x * NC + c, zz, NZ * NX + zz))
        attend(kvb, SLOT_B_LANE, picks)

        @pl.when(i > 0)
        def _():
            give_b(2 * i - 2)
            give_b(2 * i - 1)

        return carry

    between = {
        0: [lambda: both(bx_far, 0), lambda: both(bx_far, 1)],
        1: [lambda: both(cy_from, 0), lambda: both(bx_far, 2)],
        2: [lambda: both(cy_from, 1), lambda: both(bx_far, 3)],
        3: [lambda: both(cy_from, 2)],
        4: [lambda: both(cy_from, 3)],
        5: [lambda: both(cy_far, 0), lambda: both(cy_far, 1)],
        6: [lambda: both(cy_far, 2), lambda: both(cy_far, 3)],
    }
    def group(g):
        o = (4, 3, 5, 2, 6, 1, 7, 0)[g]
        zz = rem(z + o, NZ)
        if o == 0:
            wait(qv.at[pl.ds(0, NX - 1)], r_q.at[0])
            wait(qv.at[0], l_q.at[0])
        else:
            wait(qv.at[pl.ds(zz * NX, NX)], r_q.at[o])
        lax.fori_loop(g * NX // 2, (g + 1) * NX // 2, work_a, 0)

    for g in range(NZ - 1):
        group(g)
        for event in between.get(g, []):
            event()
    give_a(jnp.int32(2 * LAST - 2))
    give_a(jnp.int32(2 * LAST - 1))

    wait(qv.at[NZ * NX], l_q.at[1])
    wait(qv.at[pl.ds(NZ * NX, NZ - 1)], r_qb)
    wait(kvb.at[pl.ds(0, NBLOCKS // 2)], r_bs)
    lax.fori_loop(0, NZ // 2, work_b, 0)
    give_b(jnp.int32(NZ - 2))
    give_b(jnp.int32(NZ - 1))
    group(NZ - 1)
    give_a(jnp.int32(NZ * NX - 2))
    give_a(jnp.int32(NZ * NX - 1))

    units = NZ * NX + NZ
    wait(qv.at[pl.ds(0, units - 2)], r_o)
    wait(qv.at[pl.ds(0, 2)], l_o)
    wait(qv.at[pl.ds(0, units - 2)], s_o)
    wait(qv.at[pl.ds(0, units - 2)], s_q)
    wait(meta_v.at[pl.ds(0, NZ - 1)], s_m)
    wait(kva.at[pl.ds(0, units - 2)], s_1)
    wait(kva.at[pl.ds(0, sent["a"])], s_a)
    wait(kvb.at[pl.ds(0, sent["b"])], s_b)


def body(queries, keys, values, block_lists, block_counts):
    zz, rest = block_lists // (NY * NX * NC), block_lists % (NY * NX * NC)
    yy, rest = rest // (NX * NC), rest % (NX * NC)
    xx, cc = rest // NC, rest % NC
    slot_a = ((yy * NC + cc) * NZ + zz) * NX + xx
    slot_b = ((xx * NC + cc) * NY + yy) * NZ + zz
    rows = block_lists.shape[0]
    gap = jnp.zeros((rows, SLOT_B_LANE - LIST_LEN), jnp.int32)
    meta = jnp.concatenate(
        [slot_a, gap, slot_b, gap, block_counts[:, None], jnp.zeros((rows, 128 - COUNT_LANE - 1), jnp.int32)], axis=1
    )
    dma = pltpu.SemaphoreType.DMA
    units = NZ * NX + NZ
    return pl.pallas_call(
        kernel,
        out_shape=jax.ShapeDtypeStruct(queries.shape, jnp.bfloat16),
        in_specs=[pl.BlockSpec(memory_space=pl.ANY)] * 4,
        out_specs=pl.BlockSpec(memory_space=pl.ANY),
        scratch_shapes=[
            pltpu.VMEM((NBLOCKS, 2, BL, HD), jnp.bfloat16),
            pltpu.VMEM((NBLOCKS, 2, BL, HD), jnp.bfloat16),
            pltpu.VMEM((units, BL, HD), jnp.bfloat16),
            pltpu.VMEM((units, BL, HD), jnp.bfloat16),
            pltpu.VMEM((NZ, NX * NC, 128), jnp.int32),
            pltpu.SMEM((NZ, NX * NC, 128), jnp.int32),
            pltpu.VMEM((2, LIST_LEN // 2, BL, 2 * BL), jnp.float32),
            dma((2,)), dma((2,)), dma, dma, dma,
            dma, dma, dma, dma, dma, dma,
            dma((NZ,)), dma((NZ,)), dma((NZ,)), dma, dma, dma,
            dma((2, NZ)), dma((NZ,)), dma,
            dma((2,)), dma((2,)), dma, dma((2, 3)), dma((2, 2)), dma((2, 4)),
            dma((2,)), dma((2,)), dma((2, 4)), dma((2, 4)),
        ],
        compiler_params=pltpu.CompilerParams(collective_id=0, has_side_effects=True, vmem_limit_bytes=52 << 20),
    )(queries, keys, values, meta)


def solution(mesh):
    placed = (
        P(("seq", "uly"), None),
        P(("seq", "uly"), None),
        P(("seq", "uly"), None),
        P("seq", None),
        P("seq"),
    )
    return jax.shard_map(
        body, mesh=mesh, in_specs=placed, out_specs=P(("seq", "uly"), None), check_vma=False
    )
```

time: 159 us -> 140 us (0.88)
  Pallas kernels: 156 us -> 138 us
    pallas_call x1, Pallas kernels: 156 us -> 138 us  [body(): pl.pallas_call(kernel, out_shape=jax.ShapeDtypeStruct(queries.shape, jnp....]
where the time goes in v2:
time: 140 us
  Pallas kernels  138 us (99%)
  local copies, waits for them, and re-layouts  1.87 us (1%)
    pallas_call x1, Pallas kernels, body(): pl.pallas_call(kernel, out_shape=jax.ShapeDtypeStruct(queries.shape, jnp....  138 us

profile of v2, /device:TPU:1, one launch (start us, length us, event | category | flops | bytes accessed | tf_op | source)
XLA Modules:
  0.0 140.2 jit_solution(8727141508295693606)
XLA Ops:
  0.0 0.7 copy.6
  0.7 0.7 multiply_add_fusion
  1.5 0.1 concatenate.3.meta_ref
  1.5 137.6 %shard_map.55 = bf16[128,5120]{1,0:T(8,128)(2,1)S(1)} custom-call(bf16[128,5120]{1,0:T(8,128)(2,1)} %q_ref.1, bf16[128,5120]{1,0:T(8,128)(2,1)} %k_ref.1, bf16[128,5120]{1,0:T(8,128)(2,1)} %v_ref.1, s32[8,128]{1,0:T(8,128)S(1)} %concatenate.3.meta_ref), custom_call_target="tpu_custom_call" | custom-call | tf_op jit(solution)/shard_map/pallas_call | solution.py:466
  139.1 1.1 copy.8
  (2 shorter events, 0.0 us)

commit v3 on v2

--- a/solution.py
+++ b/solution.py
@@ -17,7 +17,7 @@
 NEAR = 2
 LAST = (NZ - 1) * NX // 2
 SLOT_B_LANE = 16
-COUNT_LANE = 32
+COUNT_ROW = NX * NC
 
 
 def rem(a, n):
@@ -235,8 +235,6 @@
         remote(v_ref.at[:, cols(h)], kvb.at[there, 1], s_1, r_b1.at[place_of(NZ - t)], target)
         return carry
 
-    lax.fori_loop(1, NZ, send_meta_b, 0)
-
     def send_a(i, carry):
         j = div(i, NX)
         t = jnp.where(j == 0, 0, step_to(j))
@@ -248,7 +246,9 @@
         remote(v_ref.at[:, cols(h)], kva.at[me_a, 1], s_1, r_a1.at[o], target)
         return carry
 
-    lax.fori_loop(1, NZ * NX, send_a, 0)
+    lax.fori_loop(1, NX, send_a, 0)
+    lax.fori_loop(1, NZ, send_meta_b, 0)
+    lax.fori_loop(NX, NZ * NX, send_a, 0)
 
     def send_q(i, carry):
         j = div(i, NX)
@@ -318,7 +318,7 @@
     key_ids = lax.broadcasted_iota(jnp.int32, (BL, 2 * BL), 1)
 
     def weigh(kv, part, row, lane, zz, unit):
-        count = meta_s[zz, row, COUNT_LANE]
+        count = meta_s[zz, COUNT_ROW, row]
         slots = [meta_s[zz, row, lane + e] for e in range(LIST_LEN)]
         if lane:
             slots = [n // NZ * NZ + place_of(rem(n % NZ + NZ - z, NZ)) for n in slots]
@@ -456,10 +456,11 @@
     xx, cc = rest // NC, rest % NC
     slot_a = ((yy * NC + cc) * NZ + zz) * NX + xx
     slot_b = ((xx * NC + cc) * NY + yy) * NZ + zz
-    rows = block_lists.shape[0]
-    gap = jnp.zeros((rows, SLOT_B_LANE - LIST_LEN), jnp.int32)
-    meta = jnp.concatenate(
-        [slot_a, gap, slot_b, gap, block_counts[:, None], jnp.zeros((rows, 128 - COUNT_LANE - 1), jnp.int32)], axis=1
+    rows = NX * NC
+    meta = (
+        jnp.pad(slot_a, ((0, rows), (0, 128 - LIST_LEN)))
+        + jnp.pad(slot_b, ((0, rows), (SLOT_B_LANE, 128 - LIST_LEN - SLOT_B_LANE)))
+        + jnp.pad(block_counts[None, :], ((rows, rows - 1), (0, 128 - rows)))
     )
     dma = pltpu.SemaphoreType.DMA
     units = NZ * NX + NZ
@@ -473,8 +474,8 @@
             pltpu.VMEM((NBLOCKS, 2, BL, HD), jnp.bfloat16),
             pltpu.VMEM((units, BL, HD), jnp.bfloat16),
             pltpu.VMEM((units, BL, HD), jnp.bfloat16),
-            pltpu.VMEM((NZ, NX * NC, 128), jnp.int32),
-            pltpu.SMEM((NZ, NX * NC, 128), jnp.int32),
+            pltpu.VMEM((NZ, 2 * NX * NC, 128), jnp.int32),
+            pltpu.SMEM((NZ, 2 * NX * NC, 128), jnp.int32),
             pltpu.VMEM((2, LIST_LEN // 2, BL, 2 * BL), jnp.float32),
             dma((2,)), dma((2,)), dma, dma, dma,
             dma, dma, dma, dma, dma, dma,

time: 140 us -> 141 us (level)
  no operation moved by 1% of the time
where the time goes in v3:
time: 141 us
  Pallas kernels  139 us (99%)
  other arithmetic  1.45 us (1%)
    pallas_call x1, Pallas kernels, body(): pl.pallas_call(kernel, out_shape=jax.ShapeDtypeStruct(queries.shape, jnp....  139 us

profile of v3, /device:TPU:1, one launch (start us, length us, event | category | flops | bytes accessed | tf_op | source)
XLA Modules:
  0.0 141.4 jit_solution(17506236482541513055)
XLA Ops:
  0.0 0.7 multiply_add_fusion.1
  0.7 0.7 pad_add_fusion.meta_ref
  1.4 138.8 %shard_map.55 = bf16[128,5120]{1,0:T(8,128)(2,1)S(1)} custom-call(bf16[128,5120]{1,0:T(8,128)(2,1)} %q_ref.1, bf16[128,5120]{1,0:T(8,128)(2,1)} %k_ref.1, bf16[128,5120]{1,0:T(8,128)(2,1)} %v_ref.1, s32[16,128]{1,0:T(8,128)S(1)} %pad_add_fusion.meta_ref), custom_call_target="tpu_custom_call" | custom-call | tf_op jit(solution)/shard_map/pallas_call | solution.py:467
  140.3 1.1 copy.7
